TPU v7x, 32 devices: a whole 2x2x4 slice. The times are simulated.
32 devices in a mesh: leaf: 4 (over x, core), front: 8 (over z, y).
Axes of the slice: x: 2, y: 2, z: 4, core: 2. Of those that a mesh axis runs over, the one named last changes fastest.
Arguments:
- leaf_field: float32 [64, 128, 4, 128], P(None, ('leaf', 'front')), may hold values from -4 to 4
- leaf_source: float32 [64, 128, 4, 128], P(None, ('leaf', 'front')), may hold values from -6 to 6
- wave_squared: float32 [128, 4, 128], P(('leaf', 'front')), may hold values from 0.5 to 3
- coupling_map: int32 [32, 512], P(('leaf', 'front')), may hold values from 0 to 255
- front_rhs: float32 [64, 2048], P(None, 'front'), may hold values from -6 to 6
- row_order: int32 [2048], P('front'), may hold values from 0 to 2047, each once
- lower_panels: bfloat16 [2048, 2048], P(None, 'front'), may hold values from -0.125 to 0.125
- inverse_slots: float32 [4096, 512], P('front'), as said below
- panel_owners: int32 [4], replicated, may hold values from 0 to 7, as said below
Outputs:
- leaf_residual: float32 [64, 128, 4, 128], P(None, ('leaf', 'front'))
- solved_blocks: float32 [64, 2048], replicated
- reduced_rhs: float32 [64, 2048], P(None, 'front')
Inputs may be any that keep to these rules, and one draw needn't show every extreme that they name: `panel_owners`: 4 distinct indices of the front axis, always including 0 and 7. `inverse_slots`: each slot of 512 rows is lower triangular with diagonal entries between 0.5 and 1.5.
All inputs are finite; a program needn't handle non-finite values.
Results may differ from a plain program's by a relative error of at most 0.0019.
Values sent between devices are 32-bit elements; how exact they have to be, the bound alone decides.
No kernel may reach another device: no remote copies, remote signals or barrier semaphores. Data moves between devices by JAX's collectives and lax.ppermute only.
A program may use at most 64 MiB of HBM per device.

v0:
```python
import jax
import jax.numpy as jnp
from jax import lax
from jax.sharding import PartitionSpec as P

centre_weight = 128.0 / 30.0
face_weight = 14.0 / 30.0
cycle_weights = (0.0, 14.0 / 30.0, 3.0 / 30.0, 1.0 / 30.0)


def spread(x, axis, root):
    mine = lax.axis_index(axis) == root
    return lax.psum(jnp.where(mine, x, jnp.zeros_like(x)), axis)


def apply_operator(field, wave):
    lead = field.ndim - 3
    padded = jnp.pad(field, [(0, 0)] * lead + [(1, 1)] * 3)
    extent_x, extent_y, extent_z = field.shape[-3:]
    beside = jnp.zeros_like(field)
    for step_x in (-1, 0, 1):
        for step_y in (-1, 0, 1):
            for step_z in (-1, 0, 1):
                distance = abs(step_x) + abs(step_y) + abs(step_z)
                if distance == 0:
                    continue
                window = padded[
                    ...,
                    1 + step_x : 1 + step_x + extent_x,
                    1 + step_y : 1 + step_y + extent_y,
                    1 + step_z : 1 + step_z + extent_z,
                ]
                beside = beside + cycle_weights[distance] * window
    return (centre_weight - wave) * field - beside


def apply_inverse(block, inverse):
    return lax.dot_general(
        block,
        inverse,
        (((1,), (1,)), ((), ())),
        precision=lax.Precision.HIGHEST,
        preferred_element_type=jnp.float32,
    )


def per_device(
    leaf_field,
    leaf_source,
    wave_squared,
    coupling_map,
    front_rhs,
    row_order,
    lower_panels,
    inverse_slots,
    panel_owners,
):
    residual = leaf_source - apply_operator(leaf_field, wave_squared)
    rhs_count = residual.shape[0]
    face = residual[:, -1].reshape(rhs_count, -1)
    rows_here = front_rhs.shape[1]
    hits = (coupling_map[0][:, None] == jnp.arange(rows_here, dtype=jnp.int32)[None, :]).astype(
        jnp.float32
    )
    coupled = face_weight * jnp.dot(
        face, hits, precision=lax.Precision.HIGHEST, preferred_element_type=jnp.float32
    )
    width = inverse_slots.shape[1]
    panel_count = lower_panels.shape[0] // width
    leading = 1.0
    reduced = front_rhs + lax.psum(coupled, "leaf")
    solved_list = []
    for panel in range(panel_count):
        wanted = panel * width + jnp.arange(width, dtype=jnp.int32)
        picker = (row_order[:, None] == wanted[None, :]).astype(jnp.float32)
        partial_block = jnp.dot(
            reduced, picker, precision=lax.Precision.HIGHEST, preferred_element_type=jnp.float32
        )
        block = lax.psum(partial_block, "front")
        own_solve = apply_inverse(block, inverse_slots)
        solved = spread(own_solve, "front", panel_owners[panel])
        solved_list.append(solved)
        solved_half = solved.astype(jnp.bfloat16)
        update = jnp.dot(
            solved_half,
            lower_panels[panel * width : (panel + 1) * width],
            preferred_element_type=jnp.float32,
        )
        keep = (row_order >= (panel + 1) * width).astype(jnp.float32)
        reduced = reduced - leading * (update * keep[None, :])
    return (residual, jnp.concatenate(solved_list, axis=1), reduced)


def solution(mesh):
    return jax.shard_map(
        per_device,
        mesh=mesh,
        in_specs=(
            P(None, ("leaf", "front"), None, None),
            P(None, ("leaf", "front"), None, None),
            P(("leaf", "front"), None, None),
            P(("leaf", "front"), None),
            P(None, "front"),
            P("front"),
            P(None, "front"),
            P("front", None),
            P(),
        ),
        out_specs=(P(None, ("leaf", "front"), None, None), P(), P(None, "front")),
        check_vma=False,
    )
```

profile of v0, /device:TPU:0, one launch (start us, length us, event | category | flops | bytes accessed | tf_op | source)
XLA Modules:
  0.0 651.4 jit_solution(8520964305867727912)
XLA Ops:
  8.0 10.8 %fusion.56 = f32[64,4,4,128]{3,2,1,0:T(4,128)S(1)} fusion(f32[64,4,4,128]{3,2,1,0:T(4,128)} %param.10, f32[64,4,4,128]{3,2,1,0:T(4,128)} %param.9, f32[4,4,128]{2,1,0:T(4,128)S(1)} %broadcast_subtract_fusion), kind=kLoop, calls=%fused_computation.91 | loop fusion | flops 7077888 | bytes 1581056 | tf_op jit(solution)/shard_map/sub | solution.py:58
  18.9 1.0 convolution_multiply_fusion
  19.9 34.3 %all-reduce.11.cloned.1.call-done = f32[64,256]{1,0:T(8,128)} async-done(((f32[64,256]{1,0:T(8,128)}), f32[64,256]{1,0:T(8,128)}) %all-reduce.11.cloned.1.call-update) | async-done | bytes 65552 | tf_op jit(solution)/shard_map/psum | solution.py:71
  54.3 0.8 add.153
  55.1 1.0 fusion.57
  57.5 71.1 %all-reduce.13.cloned.1.call-done = f32[64,512]{1,0:T(8,128)} async-done(((f32[64,512]{1,0:T(8,128)}), f32[64,512]{1,0:T(8,128)}) %all-reduce.13.cloned.1.call-update) | async-done | bytes 131088 | tf_op jit(solution)/shard_map/psum | solution.py:79
  128.6 2.7 convolution_select_fusion.3
  131.4 70.6 %all-reduce.15.cloned.1.call-done = f32[64,512]{1,0:T(8,128)} async-done(((f32[64,512]{1,0:T(8,128)}), f32[64,512]{1,0:T(8,128)}) %all-reduce.15.cloned.1.call-update) | async-done | bytes 131088 | tf_op jit(solution)/shard_map/psum | solution.py:13
  202.0 1.1 fusion.3
  203.1 1.0 fusion.62
  204.8 70.5 %all-reduce.17.cloned.1.call-done = f32[64,512]{1,0:T(8,128)} async-done(((f32[64,512]{1,0:T(8,128)}), f32[64,512]{1,0:T(8,128)}) %all-reduce.17.cloned.1.call-update) | async-done | bytes 131088 | tf_op jit(solution)/shard_map/psum | solution.py:79
  275.3 2.7 convolution_select_fusion.2
  278.1 70.5 %all-reduce.19.cloned.1.call-done = f32[64,512]{1,0:T(8,128)} async-done(((f32[64,512]{1,0:T(8,128)}), f32[64,512]{1,0:T(8,128)}) %all-reduce.19.cloned.1.call-update) | async-done | bytes 131088 | tf_op jit(solution)/shard_map/psum | solution.py:13
  348.6 1.1 fusion.2
  349.6 1.0 fusion.60
  351.4 70.4 %all-reduce.21.cloned.1.call-done = f32[64,512]{1,0:T(8,128)} async-done(((f32[64,512]{1,0:T(8,128)}), f32[64,512]{1,0:T(8,128)}) %all-reduce.21.cloned.1.call-update) | async-done | bytes 131088 | tf_op jit(solution)/shard_map/psum | solution.py:79
  421.9 2.7 convolution_select_fusion.1
  424.6 70.7 %all-reduce.23.cloned.1.call-done = f32[64,512]{1,0:T(8,128)} async-done(((f32[64,512]{1,0:T(8,128)}), f32[64,512]{1,0:T(8,128)}) %all-reduce.23.cloned.1.call-update) | async-done | bytes 131088 | tf_op jit(solution)/shard_map/psum | solution.py:13
  495.3 1.1 fusion.1
  496.5 1.0 fusion.58
  498.2 70.5 %all-reduce.25.cloned.1.call-done = f32[64,512]{1,0:T(8,128)} async-done(((f32[64,512]{1,0:T(8,128)}), f32[64,512]{1,0:T(8,128)}) %all-reduce.25.cloned.1.call-update) | async-done | bytes 131088 | tf_op jit(solution)/shard_map/psum | solution.py:79
  568.7 2.7 convolution_select_fusion
  571.4 70.7 %all-reduce.27.cloned.1.call-done = f32[64,512]{1,0:T(8,128)} async-done(((f32[64,512]{1,0:T(8,128)}), f32[64,512]{1,0:T(8,128)}) %all-reduce.27.cloned.1.call-update) | async-done | bytes 131088 | tf_op jit(solution)/shard_map/psum | solution.py:13
  642.2 1.8 pad_maximum_fusion
  (48 shorter events, 2.9 us)
Async XLA Ops:
  7.2 121.4 %copy-start = (f32[512,512]{1,0:T(8,128)S(1)}, f32[512,512]{1,0:T(8,128)}, u32[]{:S(2)}) copy-start(f32[512,512]{1,0:T(8,128)} %param.16) | copy-start | bytes 3145732
  7.2 11.7 %copy-start.10 = (s32[1,512]{1,0:T(1,128)S(1)}, s32[1,512]{1,0:T(1,128)}, u32[]{:S(2)}) copy-start(s32[1,512]{1,0:T(1,128)} %param.12) | copy-start | bytes 6148
  7.2 47.1 %all-reduce.11.cloned.1.call-start = ((), (), s32[]{:S(2)}) async-start(), calls=%async_computation | async-start | bytes 131072 | tf_op jit(solution)/shard_map/psum | solution.py:71
  8.0 46.2 %copy-start.7 = (f32[64,256]{1,0:T(8,128)S(1)}, f32[64,256]{1,0:T(8,128)}, u32[]{:S(2)}) copy-start(f32[64,256]{1,0:T(8,128)} %param.13) | copy-start | bytes 196612
  8.0 47.1 %copy-start.8 = (s32[256]{0:T(256)S(1)}, s32[256]{0:T(256)}, u32[]{:S(2)}) copy-start(s32[256]{0:T(256)} %param.14) | copy-start | bytes 3076
  8.0 48.2 %copy-start.9 = (s32[4]{0:T(128)S(1)}, s32[4]{0:T(128)}, u32[]{:S(2)}) copy-start(s32[4]{0:T(128)} %param.17) | copy-start | bytes 52
  18.8 112.5 %copy-start.2 = (f32[64,4,4,128]{3,2,1,0:T(4,128)}, f32[64,4,4,128]{3,2,1,0:T(4,128)S(1)}, u32[]{:S(2)}) copy-start(f32[64,4,4,128]{3,2,1,0:T(4,128)S(1)} %fusion.56) | copy-start | bytes 1572868
  19.9 182.2 %copy-start.1 = (bf16[2048,256]{1,0:T(8,128)(2,1)S(1)}, bf16[2048,256]{1,0:T(8,128)(2,1)}, u32[]{:S(2)}) copy-start(bf16[2048,256]{1,0:T(8,128)(2,1)} %param.15) | copy-start | bytes 3145732
  19.9 108.7 %all-reduce.13.cloned.1.call-start = ((), (), s32[]{:S(2)}) async-start(), calls=%async_computation.1 | async-start | bytes 262144 | tf_op jit(solution)/shard_map/psum | solution.py:79
  56.2 145.8 %all-reduce.15.cloned.1.call-start = ((), (), s32[]{:S(2)}) async-start(), calls=%async_computation.2 | async-start | bytes 262144 | tf_op jit(solution)/shard_map/psum | solution.py:13
  131.3 144.0 %all-reduce.17.cloned.1.call-start = ((), (), s32[]{:S(2)}) async-start(), calls=%async_computation.3 | async-start | bytes 262144 | tf_op jit(solution)/shard_map/psum | solution.py:79
  204.2 144.4 %all-reduce.19.cloned.1.call-start = ((), (), s32[]{:S(2)}) async-start(), calls=%async_computation.4 | async-start | bytes 262144 | tf_op jit(solution)/shard_map/psum | solution.py:13
  278.0 143.8 %all-reduce.21.cloned.1.call-start = ((), (), s32[]{:S(2)}) async-start(), calls=%async_computation.5 | async-start | bytes 262144 | tf_op jit(solution)/shard_map/psum | solution.py:79
  350.7 144.6 %all-reduce.23.cloned.1.call-start = ((), (), s32[]{:S(2)}) async-start(), calls=%async_computation.6 | async-start | bytes 262144 | tf_op jit(solution)/shard_map/psum | solution.py:13
  424.6 144.2 %all-reduce.25.cloned.1.call-start = ((), (), s32[]{:S(2)}) async-start(), calls=%async_computation.7 | async-start | bytes 262144 | tf_op jit(solution)/shard_map/psum | solution.py:79
  495.3 146.9 %copy-start.3 = (f32[64,512]{1,0:T(8,128)S(1)}, f32[64,512]{1,0:T(8,128)}, u32[]{:S(2)}) copy-start(f32[64,512]{1,0:T(8,128)} %all-reduce.15.cloned.1.call-done) | copy-start | bytes 393220
  495.3 146.9 %copy-start.4 = (f32[64,512]{1,0:T(8,128)S(1)}, f32[64,512]{1,0:T(8,128)}, u32[]{:S(2)}) copy-start(f32[64,512]{1,0:T(8,128)} %all-reduce.19.cloned.1.call-done) | copy-start | bytes 393220
  495.3 146.9 %copy-start.5 = (f32[64,512]{1,0:T(8,128)S(1)}, f32[64,512]{1,0:T(8,128)}, u32[]{:S(2)}) copy-start(f32[64,512]{1,0:T(8,128)} %all-reduce.23.cloned.1.call-done) | copy-start | bytes 393220
  497.5 144.7 %all-reduce.27.cloned.1.call-start = ((), (), s32[]{:S(2)}) async-start(), calls=%async_computation.8 | async-start | bytes 262144 | tf_op jit(solution)/shard_map/psum | solution.py:13
  642.2 1.8 copy-start.6
Sparse Core Ops, SparseCore 0:
  20.0 34.1 all-reduce.10
  58.2 70.3 all-reduce.12
  132.5 69.4 all-reduce.14
  205.8 69.4 all-reduce.16
  279.1 69.4 all-reduce.18
  352.3 69.4 all-reduce.20
  425.8 69.4 all-reduce.22
  499.2 69.4 all-reduce.24
  572.7 69.4 all-reduce.26
where the time goes:
time: 652 us; the launch traced here: 651 us
  waiting for transfers between devices  600 us (92%)
  matrix products  20 us (3%)
  between operations  16.5 us (3%)
  other arithmetic  14.2 us (2%)
    psum x4, waiting for transfers between devices, spread(): return lax.psum(jnp.where(mine, x, jnp.zeros_like(x)), axis)  283 us
    psum x4, waiting for transfers between devices, per_device(): block = lax.psum(partial_block, 'front')  283 us
    psum x1, waiting for transfers between devices, per_device(): reduced = front_rhs + lax.psum(coupled, 'leaf')  34.3 us
  transfers between devices with their start and end apart: 9, of which 9 were waited for; matrix products, arithmetic and copies ran while one was open for 0% of the time, Pallas kernels for 0%

commit v1 on v0

--- a/solution.py
+++ b/solution.py
@@ -76,7 +76,8 @@
         partial_block = jnp.dot(
             reduced, picker, precision=lax.Precision.HIGHEST, preferred_element_type=jnp.float32
         )
-        block = lax.psum(partial_block, "front")
+        parts = lax.all_gather(partial_block, "front")
+        block = jnp.sum(parts, axis=0)
         own_solve = apply_inverse(block, inverse_slots)
         solved = spread(own_solve, "front", panel_owners[panel])
         solved_list.append(solved)

time: 652 us -> 526 us (0.81)
  waiting for transfers between devices: 600 us -> 471 us
    psum x4 -> x0, waiting for transfers between devices: 283 us -> none  [per_device(): block = lax.psum(partial_block, 'front')]
    all_gather x0 -> x4, waiting for transfers between devices: none -> 157 us  [per_device(): parts = lax.all_gather(partial_block, 'front')]
where the time goes in v1:
time: 526 us; the launch traced here: 525 us
  waiting for transfers between devices  471 us (90%)
  other arithmetic  20.4 us (4%)
  between operations  16.4 us (3%)
  matrix products  16.3 us (3%)
    psum x4, waiting for transfers between devices, spread(): return lax.psum(jnp.where(mine, x, jnp.zeros_like(x)), axis)  279 us
    all_gather x4, waiting for transfers between devices, per_device(): parts = lax.all_gather(partial_block, 'front')  157 us
    psum x1, waiting for transfers between devices, per_device(): reduced = front_rhs + lax.psum(coupled, 'leaf')  34.3 us
    sub x1, other arithmetic, per_device(): residual = leaf_source - apply_operator(leaf_field, wave_squared)  11.6 us
  transfers between devices with their start and end apart: 9, of which 9 were waited for; matrix products, arithmetic and copies ran while one was open for 0% of the time, Pallas kernels for 0%

profile of v1, /device:TPU:0, one launch (start us, length us, event | category | flops | bytes accessed | tf_op | source)
XLA Modules:
  0.0 525.4 jit_solution(6513122682947617114)
XLA Ops:
  8.0 11.6 %fusion.56 = f32[64,4,4,128]{3,2,1,0:T(4,128)S(1)} fusion(f32[64,4,4,128]{3,2,1,0:T(4,128)} %param.10, f32[64,4,4,128]{3,2,1,0:T(4,128)} %param.9, f32[4,4,128]{2,1,0:T(4,128)S(1)} %broadcast_subtract_fusion), kind=kLoop, calls=%fused_computation.91 | loop fusion | flops 7077888 | bytes 1581056 | tf_op jit(solution)/shard_map/sub | solution.py:58
  20.7 34.3 %all-reduce.7.cloned.1.call-done = f32[64,256]{1,0:T(8,128)} async-done(((f32[64,256]{1,0:T(8,128)}), f32[64,256]{1,0:T(8,128)}) %all-reduce.7.cloned.1.call-update) | async-done | bytes 65552 | tf_op jit(solution)/shard_map/psum | solution.py:71
  58.4 39.7 %all-gather.9.cloned.1.call-done = f32[512,512]{1,0:T(8,128)} async-done(((f32[64,512]{1,0:T(8,128)}), f32[512,512]{1,0:T(8,128)}) %all-gather.9.cloned.1.call-update) | async-done | bytes 1048592 | tf_op jit(solution)/shard_map/all_gather | solution.py:79
  98.0 1.4 reduce_sum.36
  99.5 1.8 convolution_select_fusion.3
  101.3 69.8 %all-reduce.9.cloned.1.call-done = f32[64,512]{1,0:T(8,128)} async-done(((f32[64,512]{1,0:T(8,128)}), f32[64,512]{1,0:T(8,128)}) %all-reduce.9.cloned.1.call-update) | async-done | bytes 131088 | tf_op jit(solution)/shard_map/psum | solution.py:13
  171.1 1.1 fusion.3
  172.2 1.0 fusion.62
  173.9 39.2 %all-gather.11.cloned.1.call-done = f32[512,512]{1,0:T(8,128)} async-done(((f32[64,512]{1,0:T(8,128)}), f32[512,512]{1,0:T(8,128)}) %all-gather.11.cloned.1.call-update) | async-done | bytes 1048592 | tf_op jit(solution)/shard_map/all_gather | solution.py:79
  213.1 1.3 reduce_sum.37
  214.4 1.8 convolution_select_fusion.2
  216.3 69.8 %all-reduce.11.cloned.1.call-done = f32[64,512]{1,0:T(8,128)} async-done(((f32[64,512]{1,0:T(8,128)}), f32[64,512]{1,0:T(8,128)}) %all-reduce.11.cloned.1.call-update) | async-done | bytes 131088 | tf_op jit(solution)/shard_map/psum | solution.py:13
  286.0 1.1 fusion.2
  287.1 1.0 fusion.60
  288.8 39.2 %all-gather.13.cloned.1.call-done = f32[512,512]{1,0:T(8,128)} async-done(((f32[64,512]{1,0:T(8,128)}), f32[512,512]{1,0:T(8,128)}) %all-gather.13.cloned.1.call-update) | async-done | bytes 1048592 | tf_op jit(solution)/shard_map/all_gather | solution.py:79
  328.0 1.3 reduce_sum.38
  329.3 1.8 convolution_select_fusion.1
  331.2 69.9 %all-reduce.13.cloned.1.call-done = f32[64,512]{1,0:T(8,128)} async-done(((f32[64,512]{1,0:T(8,128)}), f32[64,512]{1,0:T(8,128)}) %all-reduce.13.cloned.1.call-update) | async-done | bytes 131088 | tf_op jit(solution)/shard_map/psum | solution.py:13
  401.1 1.1 fusion.1
  403.9 39.3 %all-gather.15.cloned.1.call-done = f32[512,512]{1,0:T(8,128)} async-done(((f32[64,512]{1,0:T(8,128)}), f32[512,512]{1,0:T(8,128)}) %all-gather.15.cloned.1.call-update) | async-done | bytes 1048592 | tf_op jit(solution)/shard_map/all_gather | solution.py:79
  443.2 1.4 reduce_sum.39
  444.5 1.8 convolution_select_fusion
  446.3 69.9 %all-reduce.15.cloned.1.call-done = f32[64,512]{1,0:T(8,128)} async-done(((f32[64,512]{1,0:T(8,128)}), f32[64,512]{1,0:T(8,128)}) %all-reduce.15.cloned.1.call-update) | async-done | bytes 131088 | tf_op jit(solution)/shard_map/psum | solution.py:13
  516.3 1.8 pad_maximum_fusion
  (52 shorter events, 6.8 us)
Async XLA Ops:
  7.2 92.3 %copy-start = (f32[512,512]{1,0:T(8,128)S(1)}, f32[512,512]{1,0:T(8,128)}, u32[]{:S(2)}) copy-start(f32[512,512]{1,0:T(8,128)} %param.16) | copy-start | bytes 3145732
  7.2 12.5 %copy-start.10 = (s32[1,512]{1,0:T(1,128)S(1)}, s32[1,512]{1,0:T(1,128)}, u32[]{:S(2)}) copy-start(s32[1,512]{1,0:T(1,128)} %param.12) | copy-start | bytes 6148
  7.2 47.8 %all-reduce.7.cloned.1.call-start = ((), (), s32[]{:S(2)}) async-start(), calls=%async_computation | async-start | bytes 131072 | tf_op jit(solution)/shard_map/psum | solution.py:71
  8.0 47.0 %copy-start.7 = (f32[64,256]{1,0:T(8,128)S(1)}, f32[64,256]{1,0:T(8,128)}, u32[]{:S(2)}) copy-start(f32[64,256]{1,0:T(8,128)} %param.13) | copy-start | bytes 196612
  8.0 47.9 %copy-start.8 = (s32[256]{0:T(256)S(1)}, s32[256]{0:T(256)}, u32[]{:S(2)}) copy-start(s32[256]{0:T(256)} %param.14) | copy-start | bytes 3076
  8.0 49.0 %copy-start.9 = (s32[4]{0:T(128)S(1)}, s32[4]{0:T(128)}, u32[]{:S(2)}) copy-start(s32[4]{0:T(128)} %param.17) | copy-start | bytes 52
  19.6 79.9 %copy-start.2 = (f32[64,4,4,128]{3,2,1,0:T(4,128)}, f32[64,4,4,128]{3,2,1,0:T(4,128)S(1)}, u32[]{:S(2)}) copy-start(f32[64,4,4,128]{3,2,1,0:T(4,128)S(1)} %fusion.56) | copy-start | bytes 1572868
  20.7 77.4 %all-gather.9.cloned.1.call-start = ((), (), s32[]{:S(2)}) async-start(), calls=%async_computation.5 | async-start | bytes 1179648 | tf_op jit(solution)/shard_map/all_gather | solution.py:79
  57.0 114.2 %all-reduce.9.cloned.1.call-start = ((), (), s32[]{:S(2)}) async-start(), calls=%async_computation.1 | async-start | bytes 262144 | tf_op jit(solution)/shard_map/psum | solution.py:13
  98.0 73.1 %copy-start.1 = (bf16[2048,256]{1,0:T(8,128)(2,1)S(1)}, bf16[2048,256]{1,0:T(8,128)(2,1)}, u32[]{:S(2)}) copy-start(bf16[2048,256]{1,0:T(8,128)(2,1)} %param.15) | copy-start | bytes 3145732
  101.3 111.8 %all-gather.11.cloned.1.call-start = ((), (), s32[]{:S(2)}) async-start(), calls=%async_computation.6 | async-start | bytes 1179648 | tf_op jit(solution)/shard_map/all_gather | solution.py:79
  173.3 112.7 %all-reduce.11.cloned.1.call-start = ((), (), s32[]{:S(2)}) async-start(), calls=%async_computation.2 | async-start | bytes 262144 | tf_op jit(solution)/shard_map/psum | solution.py:13
  216.2 111.8 %all-gather.13.cloned.1.call-start = ((), (), s32[]{:S(2)}) async-start(), calls=%async_computation.7 | async-start | bytes 1179648 | tf_op jit(solution)/shard_map/all_gather | solution.py:79
  288.2 112.9 %all-reduce.13.cloned.1.call-start = ((), (), s32[]{:S(2)}) async-start(), calls=%async_computation.3 | async-start | bytes 262144 | tf_op jit(solution)/shard_map/psum | solution.py:13
  331.1 112.1 %all-gather.15.cloned.1.call-start = ((), (), s32[]{:S(2)}) async-start(), calls=%async_computation.8 | async-start | bytes 1179648 | tf_op jit(solution)/shard_map/all_gather | solution.py:79
  403.2 113.1 %all-reduce.15.cloned.1.call-start = ((), (), s32[]{:S(2)}) async-start(), calls=%async_computation.4 | async-start | bytes 262144 | tf_op jit(solution)/shard_map/psum | solution.py:13
  443.2 73.1 %copy-start.3 = (f32[64,512]{1,0:T(8,128)S(1)}, f32[64,512]{1,0:T(8,128)}, u32[]{:S(2)}) copy-start(f32[64,512]{1,0:T(8,128)} %all-reduce.9.cloned.1.call-done) | copy-start | bytes 393220
  443.2 73.1 %copy-start.4 = (f32[64,512]{1,0:T(8,128)S(1)}, f32[64,512]{1,0:T(8,128)}, u32[]{:S(2)}) copy-start(f32[64,512]{1,0:T(8,128)} %all-reduce.11.cloned.1.call-done) | copy-start | bytes 393220
  443.2 73.1 %copy-start.5 = (f32[64,512]{1,0:T(8,128)S(1)}, f32[64,512]{1,0:T(8,128)}, u32[]{:S(2)}) copy-start(f32[64,512]{1,0:T(8,128)} %all-reduce.13.cloned.1.call-done) | copy-start | bytes 393220
  516.3 1.8 copy-start.6
Sparse Core Ops, SparseCore 0:
  20.8 34.1 all-reduce.6
  57.7 40.2 all-gather.8
  102.0 69.1 all-reduce.8
  173.7 39.3 all-gather.10
  216.9 69.1 all-reduce.10
  288.6 39.3 all-gather.12
  331.9 69.1 all-reduce.12
  403.8 39.3 all-gather.14
  447.1 69.1 all-reduce.14
